TPU v7x, 32 devices: a whole 2x2x4 slice. The times are simulated.
32 devices in a mesh: db: 8 (over z, x), pb: 4 (over y, core).
Axes of the slice: x: 2, y: 2, z: 4, core: 2. Of those that a mesh axis runs over, the one named last changes fastest.
Arguments:
- queries: bfloat16 [256, 4096], P('pb'), may hold values from -6 to 6
- database: bfloat16 [8192, 4096], P(('db', 'pb')), may hold values from -6 to 6
- slopes: int32 [5], replicated, may hold values from 1 to 6, as said below
Outputs:
- match_score: float32 [256, 8192], P(None, ('db', 'pb'))
Inputs may be any that keep to these rules, and one draw needn't show every extreme that they name: `slopes`: every slope lies in 1 to 6; one of them is 6 and one is 1.
All inputs are finite; a program needn't handle non-finite values.
Results may differ from a plain program's by a relative error of at most 0.0003.
Values may be sent and summed in bfloat16 or wider, within the bound.
A program may use at most 64 MiB of HBM per device.

v0:
```python
import jax
import jax.numpy as jnp
from jax import lax
from jax.sharding import PartitionSpec as P

SEQ = 20
RADIUS = 5
SLOPES = 5
SMAX = 6
variance_floor = 0.25


def padded_2(value, sides, width):
    for axis, dim in sides:
        count, length = (lax.axis_size(axis), value.shape[dim])
        up = [(i, (i + 1) % count) for i in range(count - 1)]
        down = [(j, i) for i, j in up]
        last = lax.slice_in_dim(value, length - width, length, axis=dim)
        leading = lax.slice_in_dim(value, 0, width, axis=dim)
        before = lax.ppermute(last, axis, up)
        after = lax.ppermute(leading, axis, down)
        value = jnp.concatenate([before, value, after], axis=dim)
    return value


def from_behind(value, axis, steps):
    count = lax.axis_size(axis)
    leading, last = (max(0, -steps), min(count, count - steps))
    return lax.ppermute(value, axis, [(source, source + steps) for source in range(leading, last)])


def band_mask(first_frame, frame_count, band_total):
    frame_ids = first_frame + jnp.arange(frame_count, dtype=jnp.int32)
    inside = jnp.logical_and(frame_ids >= 0, frame_ids < band_total)
    return inside.astype(jnp.float32)[None, :]


def contrast(extended, validity):
    out_width = extended.shape[1] - 2 * RADIUS
    masked = extended * validity
    squared = masked * masked
    first_sum = masked[:, :out_width]
    second_sum = squared[:, :out_width]
    counted = validity[:, :out_width]
    for offset in range(1, 2 * RADIUS + 1):
        first_sum = first_sum + masked[:, offset : offset + out_width]
        second_sum = second_sum + squared[:, offset : offset + out_width]
        counted = counted + validity[:, offset : offset + out_width]
    counted = jnp.maximum(counted, 1.0)
    average = first_sum / counted
    spread = second_sum / counted - average * average
    center = extended[:, RADIUS : RADIUS + out_width]
    keeper = validity[:, RADIUS : RADIUS + out_width]
    return keeper * (center - average) / jnp.sqrt(jnp.maximum(spread, variance_floor))


def lagged(field, steps, slope):
    col_pad = steps * SMAX
    padded = jnp.pad(field, ((steps, 0), (col_pad, 0)))
    begin = col_pad - steps * slope
    return lax.dynamic_slice(padded, (jnp.int32(0), begin), field.shape)


def window_sum(field, slope):
    powers = [field]
    stride = 1
    while 2 * stride <= SEQ:
        powers.append(powers[-1] + lagged(powers[-1], stride, slope))
        stride = stride * 2
    summed = None
    filled = 0
    for level in reversed(range(len(powers))):
        if SEQ >> level & 1:
            segment = powers[level] if filled == 0 else lagged(powers[level], filled, slope)
            summed = segment if summed is None else summed + segment
            filled = filled + (1 << level)
    return summed


def best_match(joined, slopes, reach):
    highest = None
    for member in range(SLOPES):
        summed = window_sum(joined, slopes[member])[:, reach:]
        highest = summed if highest is None else jnp.maximum(highest, summed)
    return highest * SEQ ** (-0.5)


def on_device(queries, database, slopes):
    frames = database.shape[0]
    scale = database.shape[1] ** (-0.5)
    reach = SMAX * (SEQ - 1)
    band_total = frames * lax.axis_size(("db", "pb"))
    similarity = (
        lax.dot_general(
            lax.all_gather(queries, "pb", axis=0, tiled=True),
            database,
            (((1,), (1,)), ((), ())),
            preferred_element_type=jnp.float32,
        )
        * scale
    )
    anchor = lax.axis_index(("db", "pb")) * frames
    extended = padded_2(similarity, ((("db", "pb"), 1),), RADIUS)
    normed = contrast(extended, band_mask(anchor - RADIUS, frames + 2 * RADIUS, band_total))
    carried = from_behind(normed[:, frames - reach :], ("db", "pb"), 1)
    joined = jnp.concatenate([carried, normed], axis=1)
    return best_match(joined, slopes, reach)


def solution(mesh):
    placed = (P("pb", None), P(("db", "pb"), None), P())
    return jax.shard_map(
        on_device, mesh=mesh, in_specs=placed, out_specs=P(None, ("db", "pb")), check_vma=False
    )
```

profile of v0, /device:TPU:7, one launch (start us, length us, event | category | flops | bytes accessed | tf_op | source)
XLA Modules:
  0.0 78.5 jit_solution(4593972485175373865)
XLA Ops:
  6.5 0.0 copy-start
  6.5 0.0 all-gather.2.cloned.1.call-start
  6.5 0.7 all-gather.2.cloned.1.call-update
  7.3 0.1 fusion.44
  7.4 24.8 %all-gather.2.cloned.1.call-done = bf16[256,4096]{1,0:T(8,128)(2,1)} async-done(((bf16[64,4096]{1,0:T(8,128)(2,1)}), bf16[256,4096]{1,0:T(8,128)(2,1)}) %all-gather.2.cloned.1.call-update) | async-done | bytes 2097168 | tf_op jit(solution)/shard_map/all_gather | solution.py:95
  32.2 0.0 copy-done
  32.2 2.3 %convolution_multiply_fusion = f32[256,256]{0,1:T(8,128)S(1)} fusion(bf16[256,4096]{1,0:T(8,128)(2,1)} %all-gather.2.cloned.1.call-done, bf16[256,4096]{1,0:T(8,128)(2,1)S(1)} %copy-done), kind=kOutput, calls=%fused_computation | convolution fusion | flops 536936448 | bytes 4456448 | tf_op jit(solution)/shard_map/dot_general | solution.py:94
  34.6 4.2 %collective-permute-start = (f32[256,5]{0,1:T(8,128)S(1)}, f32[256,5]{0,1:T(8,128)S(1)}, u32[]{:S(2)}, u32[]{:S(2)}) collective-permute-start(f32[256,5]{0,1:T(8,128)S(1)} %get-tuple-element.12), channel_id=1, source_target_pairs={{0,1},{1,2},{2,3},{3,4},{4,5},{5,6},{6,7},{7,8},{8,9},{9,10},{10,1... | collective-permute-start | bytes 15368 | tf_op jit(solution)/shard_map/ppermute | solution.py:20
  38.7 1.9 %collective-permute-start.1 = (f32[256,5]{0,1:T(8,128)S(1)}, f32[256,5]{0,1:T(8,128)S(1)}, u32[]{:S(2)}, u32[]{:S(2)}) collective-permute-start(f32[256,5]{0,1:T(8,128)S(1)} %get-tuple-element.13), channel_id=1, source_target_pairs={{1,0},{2,1},{3,2},{4,3},{5,4},{6,5},{7,6},{8,7},{9,8},{10,9},{11,1... | collective-permute-start | bytes 15368 | tf_op jit(solution)/shard_map/ppermute | solution.py:21
  40.7 0.0 collective-permute-done
  40.7 4.8 %collective-permute-done.1 = f32[256,5]{0,1:T(8,128)S(1)} collective-permute-done((f32[256,5]{0,1:T(8,128)S(1)}, f32[256,5]{0,1:T(8,128)S(1)}, u32[]{:S(2)}, u32[]{:S(2)}) %collective-permute-start.1) | collective-permute-done | bytes 5152 | tf_op jit(solution)/shard_map/ppermute | solution.py:21
  45.5 0.1 fusion.42
  45.6 0.0 copy-start.1
  45.6 0.5 fusion.34
  46.2 1.9 %collective-permute-start.2 = (f32[256,114]{0,1:T(8,128)S(1)}, f32[256,114]{0,1:T(8,128)S(1)}, u32[]{:S(2)}, u32[]{:S(2)}) collective-permute-start(f32[256,114]{0,1:T(8,128)S(1)} %slice.220), channel_id=1, source_target_pairs={{0,1},{1,2},{2,3},{3,4},{4,5},{5,6},{6,7},{7,8},{8,9},{9,10},{10,1... | collective-permute-start | bytes 350216 | tf_op jit(solution)/shard_map/ppermute | solution.py:29
  48.1 0.0 copy-done.1
  48.2 0.7 fusion.45
  67.1 0.0 collective-permute-done.2
  67.1 0.7 fusion.14
  67.8 0.2 fusion.4
  68.0 0.2 fusion.9
  68.2 0.3 fusion.2
  68.5 0.2 fusion.7
  68.7 0.2 fusion.8
  68.9 0.3 fusion
  69.2 0.2 fusion.5
  69.4 0.2 fusion.6
  69.6 1.2 %fusion.21 = f32[256,256]{0,1:T(8,128)S(1)} fusion(s32[]{:T(128)S(6)} %add.489, f32[256,370]{0,1:T(8,128)S(1)} %fusion.5, s32[]{:T(128)S(6)} %add.491, f32[256,370]{0,1:T(8,128)S(1)} %fusion.6, s32[]{:T(128)S(6)} %add.493, f32[256,370]{0,1:T(8,128)S(1)} %fusion.7, s32[]{:T(128)S(6)} %add.495, f32[256,370]{0,1:T(8,128)S(1)} %fusion.8, s32[]{:T(128)S(6)} %add.497, ...), kind=kLoop, calls=%fused_computation.49 | loop fusion | flops 983040 | bytes 5423144 | tf_op jit(solution)/shard_map/mul | solution.py:85
  70.8 0.8 %copy.4 = f32[256,256]{1,0:T(8,128)} copy(f32[256,256]{0,1:T(8,128)S(1)} %fusion.21) | data formatting | bytes 524288 | tf_op jit(solution)/shard_map/mul | solution.py:85
  (5 shorter events, 0.1 us)
Async XLA Ops:
  6.5 25.7 %copy-start = (bf16[256,4096]{1,0:T(8,128)(2,1)S(1)}, bf16[256,4096]{1,0:T(8,128)(2,1)}, u32[]{:S(2)}) copy-start(bf16[256,4096]{1,0:T(8,128)(2,1)} %param.4) | copy-start | bytes 6291460
  6.5 25.7 %all-gather.2.cloned.1.call-start = ((), (), s32[]{:S(2)}) async-start(), calls=%async_computation | async-start | bytes 2621440 | tf_op jit(solution)/shard_map/all_gather | solution.py:95
  34.6 6.1 %collective-permute-start = (f32[256,5]{0,1:T(8,128)S(1)}, f32[256,5]{0,1:T(8,128)S(1)}, u32[]{:S(2)}, u32[]{:S(2)}) collective-permute-start(f32[256,5]{0,1:T(8,128)S(1)} %get-tuple-element.12), channel_id=1, source_target_pairs={{0,1},{1,2},{2,3},{3,4},{4,5},{5,6},{6,7},{7,8},{8,9},{9,10},{10,1... | collective-permute-start | bytes 15368 | tf_op jit(solution)/shard_map/ppermute | solution.py:20
  38.7 6.8 %collective-permute-start.1 = (f32[256,5]{0,1:T(8,128)S(1)}, f32[256,5]{0,1:T(8,128)S(1)}, u32[]{:S(2)}, u32[]{:S(2)}) collective-permute-start(f32[256,5]{0,1:T(8,128)S(1)} %get-tuple-element.13), channel_id=1, source_target_pairs={{1,0},{2,1},{3,2},{4,3},{5,4},{6,5},{7,6},{8,7},{9,8},{10,9},{11,1... | collective-permute-start | bytes 15368 | tf_op jit(solution)/shard_map/ppermute | solution.py:21
  45.6 2.5 %copy-start.1 = (s32[5]{0:T(128)S(1)}, s32[5]{0:T(128)}, u32[]{:S(2)}) copy-start(s32[5]{0:T(128)} %param.5) | copy-start | bytes 64
  46.2 20.9 %collective-permute-start.2 = (f32[256,114]{0,1:T(8,128)S(1)}, f32[256,114]{0,1:T(8,128)S(1)}, u32[]{:S(2)}, u32[]{:S(2)}) collective-permute-start(f32[256,114]{0,1:T(8,128)S(1)} %slice.220), channel_id=1, source_target_pairs={{0,1},{1,2},{2,3},{3,4},{4,5},{5,6},{6,7},{7,8},{8,9},{9,10},{10,1... | collective-permute-start | bytes 350216 | tf_op jit(solution)/shard_map/ppermute | solution.py:29
Sparse Core Ops, SparseCore 0:
  8.9 23.2 all-gather.1
where the time goes:
time: 78.9 us; the launch traced here: 78.5 us
  between operations  31.8 us (40%)
  waiting for transfers between devices  30.4 us (39%)
  starting transfers between devices  8.05 us (10%)
  other arithmetic  4.36 us (6%)
  matrix products  2.33 us (3%)
  local copies, waits for them, and re-layouts  1.52 us (2%)
    all_gather x1, waiting for transfers between devices, on_device(): lax.all_gather(queries, 'pb', axis=0, tiled=True)  24.8 us
    ppermute x1, waiting for transfers between devices, padded_2(): after = lax.ppermute(leading, axis, down)  4.81 us
    ppermute x1, starting transfers between devices, padded_2(): before = lax.ppermute(last, axis, up)  4.18 us
    add x9, other arithmetic, window_sum(): powers.append(powers[-1] + lagged(powers[-1], stride, slope))  2.43 us
    dot_general x1, matrix products, on_device(): lax.dot_general(lax.all_gather(queries, 'pb', axis=0, tiled=True), databa...  2.33 us
    ppermute x1, starting transfers between devices, from_behind(): lax.ppermute(value, axis, [(source, source + steps) for source in range(l...  1.94 us
    ppermute x1, starting transfers between devices, padded_2(): after = lax.ppermute(leading, axis, down)  1.92 us
  transfers between devices with their start and end apart: 4, of which 2 were waited for; matrix products, arithmetic and copies ran while one was open for 1% of the time, Pallas kernels for 0%

commit v1 on v0

--- a/solution.py
+++ b/solution.py
@@ -8,6 +8,27 @@
 SLOPES = 5
 SMAX = 6
 variance_floor = 0.25
+
+
+def in_order(pieces, dim):
+    lengths = list(pieces.shape[1:])
+    lengths[dim] *= pieces.shape[0]
+    return jnp.moveaxis(pieces, 0, dim).reshape(lengths)
+
+
+def collected_by_bits(x, axis):
+    size, index = (lax.axis_size(axis), lax.axis_index(axis))
+    pieces, bit = (x[None], 1)
+    while bit < size:
+        other = lax.ppermute(pieces, axis, [(i, i ^ bit) for i in range(size)])
+        low = index & bit == 0
+        pieces = jnp.concatenate([jnp.where(low, pieces, other), jnp.where(low, other, pieces)])
+        bit *= 2
+    return pieces
+
+
+def collect(x, axis, dim):
+    return in_order(collected_by_bits(x, axis), dim)
 
 
 def padded_2(value, sides, width):
@@ -92,7 +113,7 @@
     band_total = frames * lax.axis_size(("db", "pb"))
     similarity = (
         lax.dot_general(
-            lax.all_gather(queries, "pb", axis=0, tiled=True),
+            collect(queries, "pb", 0),
             database,
             (((1,), (1,)), ((), ())),
             preferred_element_type=jnp.float32,

time: 78.9 us -> 69.6 us (0.88)
  between operations: 31.8 us -> 18.7 us
  other arithmetic: 4.36 us -> 8.22 us
  matrix products: 2.33 us -> 0.74 us
  starting transfers between devices: 8.05 us -> 8.97 us
    ppermute x0 -> x2, waiting for transfers between devices: none -> 26.2 us  [collected_by_bits(): other = lax.ppermute(pieces, axis, [(i, i ^ bit) for i in range(size)])]
    all_gather x1 -> x0, waiting for transfers between devices: 24.8 us -> none  [on_device(): lax.all_gather(queries, 'pb', axis=0, tiled=True)]
    select_n x0 -> x2, other arithmetic: none -> 2.63 us  [collected_by_bits(): jnp.where(low, pieces, other)]
    dot_general x1, matrix products: 2.33 us -> 0.74 us  [on_device(): lax.dot_general(collect(queries, 'pb', 0), database, (((1,), (1,)), ((),...]
    concatenate x0 -> x2, other arithmetic: none -> 1.26 us  [collected_by_bits(): jnp.concatenate([jnp.where(low, pieces, other), jnp.where(low, other, pie...]
    ppermute x0 -> x2, starting transfers between devices: none -> 0.9 us  [collected_by_bits(): other = lax.ppermute(pieces, axis, [(i, i ^ bit) for i in range(size)])]
  transfers between devices with their start and end apart: 4 -> 5, of which waited for: 2 -> 3; matrix products, arithmetic and copies ran while one was open for 1% -> 1% of each run, Pallas kernels for 0% -> 0%
where the time goes in v1:
time: 69.6 us; the launch traced here: 69.2 us
  waiting for transfers between devices  31.1 us (45%)
  between operations  18.7 us (27%)
  starting transfers between devices  8.97 us (13%)
  other arithmetic  8.22 us (12%)
  local copies, waits for them, and re-layouts  1.51 us (2%)
  matrix products  0.74 us (1%)
    ppermute x2, waiting for transfers between devices, collected_by_bits(): other = lax.ppermute(pieces, axis, [(i, i ^ bit) for i in range(size)])  26.2 us
    ppermute x1, waiting for transfers between devices, padded_2(): after = lax.ppermute(leading, axis, down)  4.82 us
    ppermute x1, starting transfers between devices, padded_2(): before = lax.ppermute(last, axis, up)  4.2 us
    select_n x2, other arithmetic, collected_by_bits(): jnp.where(low, pieces, other)  2.63 us
    add x9, other arithmetic, window_sum(): powers.append(powers[-1] + lagged(powers[-1], stride, slope))  2.41 us
    ppermute x1, starting transfers between devices, from_behind(): lax.ppermute(value, axis, [(source, source + steps) for source in range(l...  1.94 us
    ppermute x1, starting transfers between devices, padded_2(): after = lax.ppermute(leading, axis, down)  1.92 us
  transfers between devices with their start and end apart: 5, of which 3 were waited for; matrix products, arithmetic and copies ran while one was open for 1% of the time, Pallas kernels for 0%

profile of v1, /device:TPU:7, one launch (start us, length us, event | category | flops | bytes accessed | tf_op | source)
XLA Modules:
  0.0 69.2 jit_solution(15185940197901406751)
XLA Ops:
  0.0 0.0 copy-start
  0.0 0.7 collective-permute-start
  0.7 1.9 %collective-permute-done = bf16[1,64,4096]{2,1,0:T(8,128)(2,1)} collective-permute-done((bf16[1,64,4096]{2,1,0:T(8,128)(2,1)}, bf16[1,64,4096]{2,1,0:T(8,128)(2,1)}, u32[]{:S(2)}, u32[]{:S(2)}) %collective-permute-start) | collective-permute-done | bytes 524320 | tf_op jit(solution)/shard_map/ppermute | solution.py:23
  2.6 1.3 %broadcast_select_fusion.3 = (bf16[1,64,4096]{2,1,0:T(8,128)(2,1)S(1)}, bf16[1,64,4096]{2,1,0:T(8,128)(2,1)S(1)}) fusion(bf16[1,64,4096]{2,1,0:T(8,128)(2,1)} %collective-permute-done, pred[]{:T(512)S(6)} %eq.7, bf16[64,4096]{1,0:T(8,128)(2,1)} %param.3), kind=kLoop, calls=%fused_computation.31 | loop fusion | flops 524288 | bytes 2097153 | tf_op jit(solution)/shard_map/jit(_where)/select_n | solution.py:25
  3.8 1.1 %pad_maximum_fusion.1 = bf16[2,64,4096]{2,1,0:T(8,128)(2,1)} fusion(bf16[1,64,4096]{2,1,0:T(8,128)(2,1)S(1)} %get-tuple-element.10, bf16[1,64,4096]{2,1,0:T(8,128)(2,1)S(1)} %get-tuple-element.9), kind=kLoop, calls=%fused_computation.2 | loop fusion | flops 524288 | bytes 2097152 | tf_op jit(solution)/shard_map/concatenate | solution.py:25
  4.9 0.2 collective-permute-start.1
  5.1 0.1 fusion.44
  5.2 24.4 %collective-permute-done.1 = bf16[2,64,4096]{2,1,0:T(8,128)(2,1)} collective-permute-done((bf16[2,64,4096]{2,1,0:T(8,128)(2,1)}, bf16[2,64,4096]{2,1,0:T(8,128)(2,1)}, u32[]{:S(2)}, u32[]{:S(2)}) %collective-permute-start.1) | collective-permute-done | bytes 1048608 | tf_op jit(solution)/shard_map/ppermute | solution.py:23
  29.6 1.4 %broadcast_select_fusion.1 = (bf16[2,64,4096]{2,1,0:T(8,128)(2,1)S(1)}, bf16[2,64,4096]{2,1,0:T(8,128)(2,1)S(1)}) fusion(bf16[2,64,4096]{2,1,0:T(8,128)(2,1)} %collective-permute-done.1, pred[]{:T(512)S(6)} %eq.6, bf16[1,64,4096]{2,1,0:T(8,128)(2,1)S(1)} %get-tuple-element.10, bf16[1,64,4096]{2,1,0:T(8,128)(2,1)S(1)} %get-tuple-element.9), kind=kLoop, calls=%fused_computation.4 | loop fusion | flops 1572864 | bytes 4194305 | tf_op jit(solution)/shard_map/jit(_where)/select_n | solution.py:25
  31.0 0.2 pad_maximum_fusion
  31.2 0.7 %convolution_multiply_fusion = f32[256,256]{0,1:T(8,128)S(1)} fusion(bf16[256,4096]{1,0:T(8,128)(2,1)S(1)} %bitcast.58, bf16[256,4096]{1,0:T(8,128)(2,1)S(1)} %copy-done), kind=kOutput, calls=%fused_computation.1 | convolution fusion | flops 536936448 | bytes 4456448 | tf_op jit(solution)/shard_map/dot_general | solution.py:115
  31.9 4.2 %collective-permute-start.2 = (f32[256,5]{0,1:T(8,128)S(1)}, f32[256,5]{0,1:T(8,128)S(1)}, u32[]{:S(2)}, u32[]{:S(2)}) collective-permute-start(f32[256,5]{0,1:T(8,128)S(1)} %get-tuple-element.16), channel_id=1, source_target_pairs={{0,1},{1,2},{2,3},{3,4},{4,5},{5,6},{6,7},{7,8},{8,9},{9,10},{10,1... | collective-permute-start | bytes 15368 | tf_op jit(solution)/shard_map/ppermute | solution.py:41
  36.1 1.9 %collective-permute-start.3 = (f32[256,5]{0,1:T(8,128)S(1)}, f32[256,5]{0,1:T(8,128)S(1)}, u32[]{:S(2)}, u32[]{:S(2)}) collective-permute-start(f32[256,5]{0,1:T(8,128)S(1)} %get-tuple-element.17), channel_id=1, source_target_pairs={{1,0},{2,1},{3,2},{4,3},{5,4},{6,5},{7,6},{8,7},{9,8},{10,9},{11,1... | collective-permute-start | bytes 15368 | tf_op jit(solution)/shard_map/ppermute | solution.py:42
  38.1 0.0 collective-permute-done.2
  38.1 4.8 %collective-permute-done.3 = f32[256,5]{0,1:T(8,128)S(1)} collective-permute-done((f32[256,5]{0,1:T(8,128)S(1)}, f32[256,5]{0,1:T(8,128)S(1)}, u32[]{:S(2)}, u32[]{:S(2)}) %collective-permute-start.3) | collective-permute-done | bytes 5152 | tf_op jit(solution)/shard_map/ppermute | solution.py:42
  42.9 0.1 fusion.42
  43.0 0.0 copy-start.1
  43.0 0.5 fusion.34
  43.6 1.9 %collective-permute-start.4 = (f32[256,114]{0,1:T(8,128)S(1)}, f32[256,114]{0,1:T(8,128)S(1)}, u32[]{:S(2)}, u32[]{:S(2)}) collective-permute-start(f32[256,114]{0,1:T(8,128)S(1)} %slice.220), channel_id=1, source_target_pairs={{0,1},{1,2},{2,3},{3,4},{4,5},{5,6},{6,7},{7,8},{8,9},{9,10},{10,1... | collective-permute-start | bytes 350216 | tf_op jit(solution)/shard_map/ppermute | solution.py:50
  45.5 0.6 fusion.45
  64.7 0.0 collective-permute-done.4
  64.7 0.6 fusion.14
  65.4 0.3 fusion.2
  65.7 0.2 fusion.8
  65.9 0.2 fusion.7
  66.1 0.3 fusion
  66.4 0.2 fusion.6
  66.6 0.2 fusion.5
  66.8 0.2 fusion.4
  67.0 0.2 fusion.9
  67.2 1.2 %fusion.21 = f32[256,256]{0,1:T(8,128)S(1)} fusion(s32[]{:T(128)S(6)} %add.489, f32[256,370]{0,1:T(8,128)S(1)} %fusion.5, s32[]{:T(128)S(6)} %add.491, f32[256,370]{0,1:T(8,128)S(1)} %fusion.6, s32[]{:T(128)S(6)} %add.493, f32[256,370]{0,1:T(8,128)S(1)} %fusion.7, s32[]{:T(128)S(6)} %add.495, f32[256,370]{0,1:T(8,128)S(1)} %fusion.8, s32[]{:T(128)S(6)} %add.497, ...), kind=kLoop, calls=%fused_computation.55 | loop fusion | flops 983040 | bytes 5423144 | tf_op jit(solution)/shard_map/mul | solution.py:106
  68.3 0.8 %copy.4 = f32[256,256]{1,0:T(8,128)} copy(f32[256,256]{0,1:T(8,128)S(1)} %fusion.21) | data formatting | bytes 524288 | tf_op jit(solution)/shard_map/mul | solution.py:106
  (7 shorter events, 0.1 us)
Async XLA Ops:
  0.0 31.2 %copy-start = (bf16[256,4096]{1,0:T(8,128)(2,1)S(1)}, bf16[256,4096]{1,0:T(8,128)(2,1)}, u32[]{:S(2)}) copy-start(bf16[256,4096]{1,0:T(8,128)(2,1)} %param.4) | copy-start | bytes 6291460
  0.0 2.6 %collective-permute-start = (bf16[1,64,4096]{2,1,0:T(8,128)(2,1)}, bf16[1,64,4096]{2,1,0:T(8,128)(2,1)}, u32[]{:S(2)}, u32[]{:S(2)}) collective-permute-start(bf16[1,64,4096]{2,1,0:T(8,128)(2,1)} %bitcast.59), channel_id=1, source_target_pairs={{0,1},{1,0},{2,3},{3,2},{4,5},{5,4},{6,7},{7,6},{8,9},{9,8},{10,11... | collective-permute-start | bytes 1572872 | tf_op jit(solution)/shard_map/ppermute | solution.py:23
  4.9 24.7 %collective-permute-start.1 = (bf16[2,64,4096]{2,1,0:T(8,128)(2,1)}, bf16[2,64,4096]{2,1,0:T(8,128)(2,1)}, u32[]{:S(2)}, u32[]{:S(2)}) collective-permute-start(bf16[2,64,4096]{2,1,0:T(8,128)(2,1)} %pad_maximum_fusion.1), channel_id=1, source_target_pairs={{0,2},{1,3},{2,0},{3,1},{4,6},{5,7},{6,4},{7,5},{8,10},{9,11},{10,... | collective-permute-start | bytes 3145736 | tf_op jit(solution)/shard_map/ppermute | solution.py:23
  31.9 6.2 %collective-permute-start.2 = (f32[256,5]{0,1:T(8,128)S(1)}, f32[256,5]{0,1:T(8,128)S(1)}, u32[]{:S(2)}, u32[]{:S(2)}) collective-permute-start(f32[256,5]{0,1:T(8,128)S(1)} %get-tuple-element.16), channel_id=1, source_target_pairs={{0,1},{1,2},{2,3},{3,4},{4,5},{5,6},{6,7},{7,8},{8,9},{9,10},{10,1... | collective-permute-start | bytes 15368 | tf_op jit(solution)/shard_map/ppermute | solution.py:41
  36.1 6.8 %collective-permute-start.3 = (f32[256,5]{0,1:T(8,128)S(1)}, f32[256,5]{0,1:T(8,128)S(1)}, u32[]{:S(2)}, u32[]{:S(2)}) collective-permute-start(f32[256,5]{0,1:T(8,128)S(1)} %get-tuple-element.17), channel_id=1, source_target_pairs={{1,0},{2,1},{3,2},{4,3},{5,4},{6,5},{7,6},{8,7},{9,8},{10,9},{11,1... | collective-permute-start | bytes 15368 | tf_op jit(solution)/shard_map/ppermute | solution.py:42
  43.0 2.5 %copy-start.1 = (s32[5]{0:T(128)S(1)}, s32[5]{0:T(128)}, u32[]{:S(2)}) copy-start(s32[5]{0:T(128)} %param.5) | copy-start | bytes 64
  43.6 21.1 %collective-permute-start.4 = (f32[256,114]{0,1:T(8,128)S(1)}, f32[256,114]{0,1:T(8,128)S(1)}, u32[]{:S(2)}, u32[]{:S(2)}) collective-permute-start(f32[256,114]{0,1:T(8,128)S(1)} %slice.220), channel_id=1, source_target_pairs={{0,1},{1,2},{2,3},{3,4},{4,5},{5,6},{6,7},{7,8},{8,9},{9,10},{10,1... | collective-permute-start | bytes 350216 | tf_op jit(solution)/shard_map/ppermute | solution.py:50
